TPU v7x, 32 devices: a whole 2x2x4 slice. The times are simulated.
32 devices in a mesh: row: 8 (over z, core), col: 4 (over y, x).
Axes of the slice: x: 2, y: 2, z: 4, core: 2. Of those that a mesh axis runs over, the one named last changes fastest.
Arguments:
- context: bfloat16 [128, 16384], P('row', 'col'), may hold values from -6 to 6
- out_weight: bfloat16 [16384, 16384], P('col', 'row'), may hold values from -0.046875 to 0.046875
- residual: bfloat16 [128, 16384], P('col', 'row'), may hold values from -80 to 80
- teacher_gain: float32 [16384], replicated, may hold values from 0.5 to 1.5
- student_hidden: bfloat16 [128, 4096], P(('row', 'col')), may hold values from -6 to 6
- student_gain: float32 [4096], replicated, may hold values from 0.5 to 1.5
- projector: bfloat16 [4096, 16384], P(None, ('row', 'col')), may hold values from -0.09375 to 0.09375
Outputs:
- grad_proj: float32 [4096, 16384], P(None, ('row', 'col'))
- grad_gain: float32 [4096], replicated
- loss: float32 [], replicated
All inputs are finite; a program needn't handle non-finite values.
Results may differ from a plain program's by a relative error of at most 0.0065.
Values may be sent and summed in bfloat16 or wider, within the bound.
A program may use at most 64 MiB of HBM per device.

v0:
```python
import jax
import jax.numpy as jnp
from jax import lax
from jax.sharding import PartitionSpec as P

D_T = 16384
norm_eps = 1e-05


def normalize(hidden):
    widened = hidden.astype(jnp.float32)
    return widened * lax.rsqrt(jnp.mean(widened * widened, axis=1, keepdims=True) + norm_eps)


def per_device(
    context, out_weight, residual, teacher_gain, student_hidden, student_gain, projector
):
    row_index = lax.axis_index("row")
    context_all = lax.all_gather(context, "row", axis=0, tiled=True)
    out_block = out_weight.shape[1]
    summed = lax.psum_scatter(
        jnp.dot(context_all, out_weight, preferred_element_type=jnp.float32),
        "col",
        scatter_dimension=0,
        tiled=True,
    )
    summed = summed + residual.astype(jnp.float32)
    squares = lax.psum(jnp.sum(summed * summed, axis=1), "row")
    gain_block = lax.dynamic_slice_in_dim(teacher_gain, row_index * out_block, out_block)
    final_rows = (summed * lax.rsqrt(squares / D_T + norm_eps)[:, None] * gain_block).astype(
        jnp.bfloat16
    )
    target = lax.all_to_all(final_rows, "col", split_axis=1, concat_axis=0, tiled=True)
    hidden_all = lax.all_gather(student_hidden, ("row", "col"), axis=0, tiled=True)
    normed_all = normalize(hidden_all)
    student_all = (normed_all * student_gain).astype(jnp.bfloat16)
    predicted = jnp.dot(student_all, projector, preferred_element_type=jnp.float32)
    difference = predicted - target.astype(jnp.float32)
    loss_part = jnp.sum(difference * difference)
    loss_total = lax.psum(loss_part, ("row", "col"))
    error_term = (difference * (1.0 / 64.0)).astype(jnp.bfloat16)
    grad_proj = lax.dot_general(
        student_all, error_term, (((0,), (0,)), ((), ())), preferred_element_type=jnp.float32
    )
    grad_normed = lax.dot_general(
        error_term, projector, (((1,), (1,)), ((), ())), preferred_element_type=jnp.float32
    )
    gain_part = jnp.sum(grad_normed * normed_all, axis=0)
    grad_gain = lax.psum(gain_part, ("row", "col"))
    tokens_all = predicted.shape[0]
    loss = loss_total / (tokens_all * D_T)
    return (grad_proj, grad_gain, loss)


def solution(mesh):
    placed = (
        P("row", "col"),
        P("col", "row"),
        P("col", "row"),
        P(),
        P(("row", "col"), None),
        P(),
        P(None, ("row", "col")),
    )
    return jax.shard_map(
        per_device,
        mesh=mesh,
        in_specs=placed,
        out_specs=(P(None, ("row", "col")), P(), P()),
        check_vma=False,
    )
```

profile of v0, /device:TPU:12, one launch (start us, length us, event | category | flops | bytes accessed | tf_op | source)
XLA Modules:
  0.0 205.2 jit_solution(2190091404144003150)
XLA Ops:
  7.2 0.0 all-gather.4.cloned.1.call-start
  7.2 0.7 all-gather.4.cloned.1.call-update
  7.9 0.0 all-gather.6.cloned.1.call-start
  7.9 0.7 all-gather.6.cloned.1.call-update
  8.6 0.0 reduce-scatter.2.cloned.1.call-start
  8.7 24.4 %all-gather.4.cloned.1.call-done = bf16[128,4096]{1,0:T(8,128)(2,1)} async-done(((bf16[16,4096]{1,0:T(8,128)(2,1)}), bf16[128,4096]{1,0:T(8,128)(2,1)}) %all-gather.4.cloned.1.call-update) | async-done | bytes 1048592 | tf_op jit(solution)/shard_map/all_gather | solution.py:19
  33.1 9.4 %fusion.4 = f32[128,2048]{1,0:T(8,128)} fusion(bf16[128,4096]{1,0:T(8,128)(2,1)} %all-gather.4.cloned.1.call-done, bf16[4096,2048]{1,0:T(8,128)(2,1)} %param.8), kind=kOutput, calls=%fused_computation.16 | convolution fusion | flops 2147483648 | bytes 18874368 | tf_op jit(solution)/shard_map/dot_general | solution.py:22
  42.5 0.0 reduce-scatter.2.cloned.1.call-update
  42.5 0.0 copy-start.1
  42.5 0.0 dynamic-slice-start
  42.5 46.0 %all-gather.6.cloned.1.call-done = bf16[32,4,4096]{2,1,0:T(4,128)(2,1)} async-done(((bf16[1,4,4096]{2,1,0:T(4,128)(2,1)}), bf16[32,4,4096]{2,1,0:T(4,128)(2,1)}) %all-gather.6.cloned.1.call-update) | async-done | bytes 1048592 | tf_op jit(solution)/shard_map/all_gather | solution.py:34
  88.5 1.3 reshape.25
  89.8 0.0 copy-start.2
  89.8 0.2 multiply_reduce_fusion
  90.0 29.6 %reduce-scatter.2.cloned.1.call-done = f32[32,2048]{1,0:T(8,128)} async-done(((f32[128,2048]{1,0:T(8,128)}), f32[32,2048]{1,0:T(8,128)}) %reduce-scatter.2.cloned.1.call-update) | async-done | bytes 262160 | tf_op jit(solution)/shard_map/reduce_scatter | solution.py:21
  119.7 0.0 copy-done.1
  119.7 1.1 multiply_reduce_fusion.2
  120.8 12.7 %psum.21 = f32[32]{0:T(128)S(1)} all-reduce(f32[32]{0:T(128)S(1)} %multiply_reduce_fusion.2), channel_id=1, replica_groups=mesh['row'=8,'col'=4] {'row'}, use_global_device_ids=true, to_apply=%region_3.0 | all-reduce | flops 32 | bytes 256 | tf_op jit(solution)/shard_map/psum | solution.py:28
  133.4 0.0 dynamic-slice-done
  133.4 1.0 multiply_convert_fusion.2
  134.5 0.7 copy.14
  135.2 3.9 %all-to-all-start = ((bf16[32,4,512]{2,0,1:T(8,128)(2,1)}), bf16[32,4,512]{2,0,1:T(8,128)(2,1)S(1)}, u32[]{:S(2)}, u32[]{:S(2)}) async-start(bf16[32,4,512]{2,0,1:T(8,128)(2,1)} %bitcast.11), calls=%async_computation.1 | async-start | bytes 262144 | tf_op jit(solution)/shard_map/all_to_all | solution.py:33
  139.0 3.9 %all-to-all-done = bf16[32,4,512]{2,0,1:T(8,128)(2,1)S(1)} async-done(((bf16[32,4,512]{2,0,1:T(8,128)(2,1)}), bf16[32,4,512]{2,0,1:T(8,128)(2,1)S(1)}, u32[]{:S(2)}, u32[]{:S(2)}) %all-to-all-start) | async-done | bytes 131104 | tf_op jit(solution)/shard_map/all_to_all | solution.py:33
  143.0 0.0 copy-done.2
  143.0 0.0 copy-start
  143.0 3.7 %multiply_reduce_fusion.1 = (f32[]{:T(128)}, f32[128,512]{1,0:T(8,128)S(1)}) fusion(f32[128,512]{1,0:T(8,128)S(1)} %bitcast.12, bf16[4096,512]{1,0:T(8,128)(2,1)} %param.13, f32[128,4096]{1,0:T(8,128)S(1)} %reshape.25, f32[4096]{0:T(1024)S(1)} %copy-done.2, f32[128]{0:T(128)S(1)} %add_rsqrt_fusion.1), kind=kOutput, calls=%fused_computation.5 | convolution fusion | flops 538640384 | bytes 6832644 | tf_op jit(solution)/shard_map/dot_general | solution.py:37
  146.7 0.0 copy-done
  146.7 1.5 fusion
  148.2 4.8 %fusion.1 = f32[4096,512]{1,0:T(8,128)} fusion(f32[128,512]{1,0:T(8,128)S(1)} %get-tuple-element.6, f32[128,4096]{1,0:T(8,128)S(1)} %reshape.25, f32[4096]{0:T(1024)S(1)} %copy-done.2, f32[128]{0:T(128)S(1)} %add_rsqrt_fusion.1), kind=kOutput, calls=%fused_computation.11 | convolution fusion | flops 538574848 | bytes 10764800 | tf_op jit(solution)/shard_map/dot_general | solution.py:42
  153.0 43.9 %all-reduce = (f32[4096]{0:T(1024)}, f32[]{:T(128)}) all-reduce(f32[4096]{0:T(1024)S(1)} %fusion, f32[]{:T(128)} %get-tuple-element.5), channel_id=1, replica_groups=mesh['row'=8,'col'=4] {'row','col'}, use_global_device_ids=true, to_apply=%region_5.0 | all-reduce | flops 4097 | bytes 32776 | tf_op jit(solution)/shard_map/psum | solution.py:49
  (3 shorter events, 0.0 us)
Async XLA Ops:
  7.2 25.9 %all-gather.4.cloned.1.call-start = ((), (), s32[]{:S(2)}) async-start(), calls=%async_computation.2 | async-start | bytes 1179648 | tf_op jit(solution)/shard_map/all_gather | solution.py:19
  7.9 80.6 %all-gather.6.cloned.1.call-start = ((), (), s32[]{:S(2)}) async-start(), calls=%async_computation.4 | async-start | bytes 1081344 | tf_op jit(solution)/shard_map/all_gather | solution.py:34
  8.6 111.0 %reduce-scatter.2.cloned.1.call-start = ((), (), s32[]{:S(2)}) async-start(), calls=%async_computation.3 | async-start | bytes 1310720 | tf_op jit(solution)/shard_map/reduce_scatter | solution.py:21
  42.5 77.2 %copy-start.1 = (bf16[32,2048]{1,0:T(8,128)(2,1)S(1)}, bf16[32,2048]{1,0:T(8,128)(2,1)}, u32[]{:S(2)}) copy-start(bf16[32,2048]{1,0:T(8,128)(2,1)} %param.9) | copy-start | bytes 393220
  42.5 90.9 %dynamic-slice-start = ((f32[16384]{0:T(1024)}, s32[]{:T(128)}), f32[2048]{0:T(1024)S(1)}, s32[]{:S(2)}) async-start(f32[16384]{0:T(1024)} %param.10, s32[]{:T(128)} %select_n.3), calls=%async_computation.5 | async-start | bytes 16896 | tf_op jit(solution)/shard_map/dynamic_slice | solution.py:29
  89.8 53.2 %copy-start.2 = (f32[4096]{0:T(1024)S(1)}, f32[4096]{0:T(1024)}, u32[]{:S(2)}) copy-start(f32[4096]{0:T(1024)} %param.12) | copy-start | bytes 49156
  135.2 7.8 %all-to-all-start = ((bf16[32,4,512]{2,0,1:T(8,128)(2,1)}), bf16[32,4,512]{2,0,1:T(8,128)(2,1)S(1)}, u32[]{:S(2)}, u32[]{:S(2)}) async-start(bf16[32,4,512]{2,0,1:T(8,128)(2,1)} %bitcast.11), calls=%async_computation.1 | async-start | bytes 262144 | tf_op jit(solution)/shard_map/all_to_all | solution.py:33
  143.0 3.8 %copy-start = (bf16[4096,512]{1,0:T(8,128)(2,1)S(1)}, bf16[4096,512]{1,0:T(8,128)(2,1)}, u32[]{:S(2)}) copy-start(bf16[4096,512]{1,0:T(8,128)(2,1)} %param.13) | copy-start | bytes 12582916
Sparse Core Ops, SparseCore 0:
  9.6 23.4 all-gather.3
  36.1 52.4 all-gather.5
  92.0 27.6 reduce-scatter.1
where the time goes:
time: 206 us; the launch traced here: 205 us
  waiting for transfers between devices  105 us (51%)
  blocking collectives  56.6 us (27%)
  matrix products  19.4 us (9%)
  between operations  15.6 us (8%)
  starting transfers between devices  3.99 us (2%)
  other arithmetic  2.4 us (1%)
    all_gather x1, waiting for transfers between devices, per_device(): lax.all_gather(student_hidden, ('row', 'col'), axis=0, tiled=True)  46 us
    psum x1, blocking collectives, per_device(): grad_gain = lax.psum(gain_part, ('row', 'col'))  43.9 us
    reduce_scatter x1, waiting for transfers between devices, per_device(): lax.psum_scatter(jnp.dot(context_all, out_weight, preferred_element_type=...  29.6 us
    all_gather x1, waiting for transfers between devices, per_device(): context_all = lax.all_gather(context, 'row', axis=0, tiled=True)  24.4 us
    psum x1, blocking collectives, per_device(): squares = lax.psum(jnp.sum(summed * summed, axis=1), 'row')  12.7 us
    dot_general x1, matrix products, per_device(): jnp.dot(context_all, out_weight, preferred_element_type=jnp.float32)  9.41 us
    dot_general x1, matrix products, per_device(): lax.dot_general(student_all, error_term, (((0,), (0,)), ((), ())), prefer...  4.77 us
  transfers between devices with their start and end apart: 4, of which 4 were waited for; matrix products, arithmetic and copies ran while one was open for 5% of the time, Pallas kernels for 0%

commit v1 on v0

--- a/solution.py
+++ b/solution.py
@@ -16,7 +16,13 @@
     context, out_weight, residual, teacher_gain, student_hidden, student_gain, projector
 ):
     row_index = lax.axis_index("row")
-    context_all = lax.all_gather(context, "row", axis=0, tiled=True)
+    dev_n = lax.axis_size("row")
+    pile = [context]
+    for p in range(dev_n - 1):
+        pile.append(lax.ppermute(pile[-1], "row", [(q, (q + 1) % dev_n) for q in range(dev_n)]))
+    context_all = jnp.roll(
+        jnp.concatenate(pile[::-1], axis=0), (lax.axis_index("row") + 1) * context.shape[0], 0
+    )
     out_block = out_weight.shape[1]
     summed = lax.psum_scatter(
         jnp.dot(context_all, out_weight, preferred_element_type=jnp.float32),

time: 206 us -> 189 us (0.917)
  waiting for transfers between devices: 105 us -> 86.1 us
    ppermute x0 -> x7, waiting for transfers between devices: none -> 35.1 us  [per_device(): lax.ppermute(pile[-1], 'row', [(q, (q + 1) % dev_n) for q in range(dev_n)])]
    reduce_scatter x1, waiting for transfers between devices: 29.6 us -> 0.02 us  [per_device(): lax.psum_scatter(jnp.dot(context_all, out_weight, preferred_element_type=...]
    all_gather x1 -> x0, waiting for transfers between devices: 24.4 us -> none  [per_device(): context_all = lax.all_gather(context, 'row', axis=0, tiled=True)]
  transfers between devices with their start and end apart: 4 -> 10, of which waited for: 4 -> 9; matrix products, arithmetic and copies ran while one was open for 5% -> 6% of each run, Pallas kernels for 0% -> 0%
where the time goes in v1:
time: 189 us
  waiting for transfers between devices  86.1 us (46%)
  blocking collectives  56.8 us (30%)
  matrix products  19.1 us (10%)
  between operations  17.5 us (9%)
  starting transfers between devices  4 us (2%)
  local copies, waits for them, and re-layouts  3.06 us (2%)
  other arithmetic  2.4 us (1%)
    all_gather x1, waiting for transfers between devices, per_device(): lax.all_gather(student_hidden, ('row', 'col'), axis=0, tiled=True)  47.1 us
    psum x1, blocking collectives, per_device(): grad_gain = lax.psum(gain_part, ('row', 'col'))  43.9 us
    ppermute x7, waiting for transfers between devices, per_device(): lax.ppermute(pile[-1], 'row', [(q, (q + 1) % dev_n) for q in range(dev_n)])  35.1 us
    psum x1, blocking collectives, per_device(): squares = lax.psum(jnp.sum(summed * summed, axis=1), 'row')  12.9 us
    dot_general x1, matrix products, per_device(): jnp.dot(context_all, out_weight, preferred_element_type=jnp.float32)  9.1 us
    dot_general x1, matrix products, per_device(): lax.dot_general(student_all, error_term, (((0,), (0,)), ((), ())), prefer...  4.77 us
    all_to_all x1, waiting for transfers between devices, per_device(): lax.all_to_all(final_rows, 'col', split_axis=1, concat_axis=0, tiled=True)  3.91 us
    all_to_all x1, starting transfers between devices, per_device(): lax.all_to_all(final_rows, 'col', split_axis=1, concat_axis=0, tiled=True)  3.85 us
  transfers between devices with their start and end apart: 10, of which 9 were waited for; matrix products, arithmetic and copies ran while one was open for 6% of the time, Pallas kernels for 0%

profile of v1, /device:TPU:12, one launch (start us, length us, event | category | flops | bytes accessed | tf_op | source)
XLA Modules:
  0.0 189.0 jit_solution(12437921234076817069)
XLA Ops:
  8.0 0.0 copy-start.2
  8.0 0.0 all-gather.3.cloned.1.call-start
  8.1 0.1 collective-permute-start
  8.1 4.6 %collective-permute-done = bf16[16,4096]{1,0:T(8,128)(2,1)S(1)} collective-permute-done((bf16[16,4096]{1,0:T(8,128)(2,1)}, bf16[16,4096]{1,0:T(8,128)(2,1)S(1)}, u32[]{:S(2)}, u32[]{:S(2)}) %collective-permute-start) | collective-permute-done | bytes 131104 | tf_op jit(solution)/shard_map/ppermute | solution.py:22
  12.7 0.0 collective-permute-start.1
  12.7 4.4 %collective-permute-done.1 = bf16[16,4096]{1,0:T(8,128)(2,1)S(1)} collective-permute-done((bf16[16,4096]{1,0:T(8,128)(2,1)S(1)}, bf16[16,4096]{1,0:T(8,128)(2,1)S(1)}, u32[]{:S(2)}, u32[]{:S(2)}) %collective-permute-start.1) | collective-permute-done | bytes 131104 | tf_op jit(solution)/shard_map/ppermute | solution.py:22
  17.1 0.0 collective-permute-start.2
  17.1 4.4 %collective-permute-done.2 = bf16[16,4096]{1,0:T(8,128)(2,1)S(1)} collective-permute-done((bf16[16,4096]{1,0:T(8,128)(2,1)S(1)}, bf16[16,4096]{1,0:T(8,128)(2,1)S(1)}, u32[]{:S(2)}, u32[]{:S(2)}) %collective-permute-start.2) | collective-permute-done | bytes 131104 | tf_op jit(solution)/shard_map/ppermute | solution.py:22
  21.5 0.0 collective-permute-start.3
  21.5 4.4 %collective-permute-done.3 = bf16[16,4096]{1,0:T(8,128)(2,1)S(1)} collective-permute-done((bf16[16,4096]{1,0:T(8,128)(2,1)S(1)}, bf16[16,4096]{1,0:T(8,128)(2,1)S(1)}, u32[]{:S(2)}, u32[]{:S(2)}) %collective-permute-start.3) | collective-permute-done | bytes 131104 | tf_op jit(solution)/shard_map/ppermute | solution.py:22
  25.9 0.0 collective-permute-start.4
  25.9 5.1 %collective-permute-done.4 = bf16[16,4096]{1,0:T(8,128)(2,1)S(1)} collective-permute-done((bf16[16,4096]{1,0:T(8,128)(2,1)S(1)}, bf16[16,4096]{1,0:T(8,128)(2,1)S(1)}, u32[]{:S(2)}, u32[]{:S(2)}) %collective-permute-start.4) | collective-permute-done | bytes 131104 | tf_op jit(solution)/shard_map/ppermute | solution.py:22
  30.9 0.0 collective-permute-start.5
  31.0 6.2 %collective-permute-done.5 = bf16[16,4096]{1,0:T(8,128)(2,1)S(1)} collective-permute-done((bf16[16,4096]{1,0:T(8,128)(2,1)S(1)}, bf16[16,4096]{1,0:T(8,128)(2,1)S(1)}, u32[]{:S(2)}, u32[]{:S(2)}) %collective-permute-start.5) | collective-permute-done | bytes 131104 | tf_op jit(solution)/shard_map/ppermute | solution.py:22
  37.1 0.0 collective-permute-start.6
  37.1 0.0 all-gather.3.cloned.1.call-update
  37.2 0.0 reduce-scatter.2.cloned.1.call-start
  37.2 6.1 %collective-permute-done.6 = bf16[16,4096]{1,0:T(8,128)(2,1)S(1)} collective-permute-done((bf16[16,4096]{1,0:T(8,128)(2,1)S(1)}, bf16[16,4096]{1,0:T(8,128)(2,1)S(1)}, u32[]{:S(2)}, u32[]{:S(2)}) %collective-permute-start.6) | collective-permute-done | bytes 131104 | tf_op jit(solution)/shard_map/ppermute | solution.py:22
  43.5 0.9 constant_dynamic-update-slice_fusion.8
  44.5 0.0 copy-done.2
  44.5 9.1 %fusion.1 = f32[128,2048]{1,0:T(8,128)} fusion(bf16[4096,2048]{1,0:T(8,128)(2,1)} %param.8, bf16[256,4096]{1,0:T(8,128)(2,1)S(1)} %constant_dynamic-update-slice_fusion, s32[]{:T(128)S(6)} %select_n.17), kind=kOutput, calls=%fused_computation.5 | convolution fusion | flops 2147483648 | bytes 18874372 | tf_op jit(solution)/shard_map/dot_general | solution.py:28
  53.6 0.0 reduce-scatter.2.cloned.1.call-update
  53.7 0.0 copy-start.1
  53.7 0.0 dynamic-slice-start
  53.7 47.1 %all-gather.3.cloned.1.call-done = bf16[32,4,4096]{2,1,0:T(4,128)(2,1)} async-done(((bf16[1,4,4096]{2,1,0:T(4,128)(2,1)}), bf16[32,4,4096]{2,1,0:T(4,128)(2,1)}) %all-gather.3.cloned.1.call-update) | async-done | bytes 1048592 | tf_op jit(solution)/shard_map/all_gather | solution.py:40
  100.7 1.3 reshape.25
  102.0 0.0 copy-start.3
  102.0 0.2 multiply_reduce_fusion
  102.3 0.0 reduce-scatter.2.cloned.1.call-done
  102.3 0.0 copy-done.1
  102.3 1.1 multiply_reduce_fusion.2
  103.4 12.9 %psum.21 = f32[32]{0:T(128)S(1)} all-reduce(f32[32]{0:T(128)S(1)} %multiply_reduce_fusion.2), channel_id=1, replica_groups=mesh['row'=8,'col'=4] {'row'}, use_global_device_ids=true, to_apply=%region_3.4 | all-reduce | flops 32 | bytes 256 | tf_op jit(solution)/shard_map/psum | solution.py:34
  116.4 0.0 dynamic-slice-done
  116.4 1.0 multiply_convert_fusion.2
  117.4 0.7 copy.14
  118.1 3.8 %all-to-all-start = ((bf16[32,4,512]{2,0,1:T(8,128)(2,1)}), bf16[32,4,512]{2,0,1:T(8,128)(2,1)S(1)}, u32[]{:S(2)}, u32[]{:S(2)}) async-start(bf16[32,4,512]{2,0,1:T(8,128)(2,1)} %bitcast.10), calls=%async_computation.1 | async-start | bytes 262144 | tf_op jit(solution)/shard_map/all_to_all | solution.py:39
  121.9 3.9 %all-to-all-done = bf16[32,4,512]{2,0,1:T(8,128)(2,1)S(1)} async-done(((bf16[32,4,512]{2,0,1:T(8,128)(2,1)}), bf16[32,4,512]{2,0,1:T(8,128)(2,1)S(1)}, u32[]{:S(2)}, u32[]{:S(2)}) %all-to-all-start) | async-done | bytes 131104 | tf_op jit(solution)/shard_map/all_to_all | solution.py:39
  125.9 0.0 copy-done.3
  125.9 0.0 copy-start
  125.9 3.7 %multiply_reduce_fusion.1 = (f32[]{:T(128)}, f32[128,512]{1,0:T(8,128)S(1)}) fusion(f32[128,512]{1,0:T(8,128)S(1)} %bitcast.11, bf16[4096,512]{1,0:T(8,128)(2,1)} %param.13, f32[128,4096]{1,0:T(8,128)S(1)} %reshape.25, f32[4096]{0:T(1024)S(1)} %copy-done.3, f32[128]{0:T(128)S(1)} %add_rsqrt_fusion.1), kind=kOutput, calls=%fused_computation.7 | convolution fusion | flops 538640384 | bytes 6832644 | tf_op jit(solution)/shard_map/dot_general | solution.py:43
  129.6 0.0 copy-done
  129.6 1.5 fusion
  131.1 4.8 %fusion.3 = f32[4096,512]{1,0:T(8,128)} fusion(f32[128,512]{1,0:T(8,128)S(1)} %get-tuple-element.6, f32[128,4096]{1,0:T(8,128)S(1)} %reshape.25, f32[4096]{0:T(1024)S(1)} %copy-done.3, f32[128]{0:T(128)S(1)} %add_rsqrt_fusion.1), kind=kOutput, calls=%fused_computation.13 | convolution fusion | flops 538574848 | bytes 10764800 | tf_op jit(solution)/shard_map/dot_general | solution.py:48
  135.9 43.9 %all-reduce = (f32[4096]{0:T(1024)}, f32[]{:T(128)}) all-reduce(f32[4096]{0:T(1024)S(1)} %fusion, f32[]{:T(128)} %get-tuple-element.5), channel_id=1, replica_groups=mesh['row'=8,'col'=4] {'row','col'}, use_global_device_ids=true, to_apply=%region_5.6 | all-reduce | flops 4097 | bytes 32776 | tf_op jit(solution)/shard_map/psum | solution.py:55
  (18 shorter events, 0.2 us)
Async XLA Ops:
  8.0 36.5 %copy-start.2 = (bf16[16,4096]{1,0:T(8,128)(2,1)S(1)}, bf16[16,4096]{1,0:T(8,128)(2,1)}, u32[]{:S(2)}) copy-start(bf16[16,4096]{1,0:T(8,128)(2,1)} %param.7) | copy-start | bytes 393220
  8.0 92.7 %all-gather.3.cloned.1.call-start = ((), (), s32[]{:S(2)}) async-start(), calls=%async_computation.3 | async-start | bytes 1081344 | tf_op jit(solution)/shard_map/all_gather | solution.py:40
  8.1 4.7 %collective-permute-start = (bf16[16,4096]{1,0:T(8,128)(2,1)}, bf16[16,4096]{1,0:T(8,128)(2,1)S(1)}, u32[]{:S(2)}, u32[]{:S(2)}) collective-permute-start(bf16[16,4096]{1,0:T(8,128)(2,1)} %param.7), channel_id=1, source_target_pairs={{0,4},{4,8},{8,12},{12,16},{16,20},{20,24},{24,28},{28,0},{1,5},{5... | collective-permute-start | bytes 393224 | tf_op jit(solution)/shard_map/ppermute | solution.py:22
  12.7 4.4 %collective-permute-start.1 = (bf16[16,4096]{1,0:T(8,128)(2,1)S(1)}, bf16[16,4096]{1,0:T(8,128)(2,1)S(1)}, u32[]{:S(2)}, u32[]{:S(2)}) collective-permute-start(bf16[16,4096]{1,0:T(8,128)(2,1)S(1)} %collective-permute-done), channel_id=1, source_target_pairs={{0,4},{4,8},{8,12},{12,16},{16,20},{20,24},{24,28},{28,0},{1,5},{5... | collective-permute-start | bytes 393224 | tf_op jit(solution)/shard_map/ppermute | solution.py:22
  17.1 4.4 %collective-permute-start.2 = (bf16[16,4096]{1,0:T(8,128)(2,1)S(1)}, bf16[16,4096]{1,0:T(8,128)(2,1)S(1)}, u32[]{:S(2)}, u32[]{:S(2)}) collective-permute-start(bf16[16,4096]{1,0:T(8,128)(2,1)S(1)} %collective-permute-done.1), channel_id=1, source_target_pairs={{0,4},{4,8},{8,12},{12,16},{16,20},{20,24},{24,28},{28,0},{1,5},{5... | collective-permute-start | bytes 393224 | tf_op jit(solution)/shard_map/ppermute | solution.py:22
  21.5 4.4 %collective-permute-start.3 = (bf16[16,4096]{1,0:T(8,128)(2,1)S(1)}, bf16[16,4096]{1,0:T(8,128)(2,1)S(1)}, u32[]{:S(2)}, u32[]{:S(2)}) collective-permute-start(bf16[16,4096]{1,0:T(8,128)(2,1)S(1)} %collective-permute-done.2), channel_id=1, source_target_pairs={{0,4},{4,8},{8,12},{12,16},{16,20},{20,24},{24,28},{28,0},{1,5},{5... | collective-permute-start | bytes 393224 | tf_op jit(solution)/shard_map/ppermute | solution.py:22
  25.9 5.1 %collective-permute-start.4 = (bf16[16,4096]{1,0:T(8,128)(2,1)S(1)}, bf16[16,4096]{1,0:T(8,128)(2,1)S(1)}, u32[]{:S(2)}, u32[]{:S(2)}) collective-permute-start(bf16[16,4096]{1,0:T(8,128)(2,1)S(1)} %collective-permute-done.3), channel_id=1, source_target_pairs={{0,4},{4,8},{8,12},{12,16},{16,20},{20,24},{24,28},{28,0},{1,5},{5... | collective-permute-start | bytes 393224 | tf_op jit(solution)/shard_map/ppermute | solution.py:22
  30.9 6.2 %collective-permute-start.5 = (bf16[16,4096]{1,0:T(8,128)(2,1)S(1)}, bf16[16,4096]{1,0:T(8,128)(2,1)S(1)}, u32[]{:S(2)}, u32[]{:S(2)}) collective-permute-start(bf16[16,4096]{1,0:T(8,128)(2,1)S(1)} %collective-permute-done.4), channel_id=1, source_target_pairs={{0,4},{4,8},{8,12},{12,16},{16,20},{20,24},{24,28},{28,0},{1,5},{5... | collective-permute-start | bytes 393224 | tf_op jit(solution)/shard_map/ppermute | solution.py:22
  37.1 6.2 %collective-permute-start.6 = (bf16[16,4096]{1,0:T(8,128)(2,1)S(1)}, bf16[16,4096]{1,0:T(8,128)(2,1)S(1)}, u32[]{:S(2)}, u32[]{:S(2)}) collective-permute-start(bf16[16,4096]{1,0:T(8,128)(2,1)S(1)} %collective-permute-done.5), channel_id=1, source_target_pairs={{0,4},{4,8},{8,12},{12,16},{16,20},{20,24},{24,28},{28,0},{1,5},{5... | collective-permute-start | bytes 393224 | tf_op jit(solution)/shard_map/ppermute | solution.py:22
  37.2 65.1 %reduce-scatter.2.cloned.1.call-start = ((), (), s32[]{:S(2)}) async-start(), calls=%async_computation.2 | async-start | bytes 1310720 | tf_op jit(solution)/shard_map/reduce_scatter | solution.py:27
  53.7 48.6 %copy-start.1 = (bf16[32,2048]{1,0:T(8,128)(2,1)S(1)}, bf16[32,2048]{1,0:T(8,128)(2,1)}, u32[]{:S(2)}) copy-start(bf16[32,2048]{1,0:T(8,128)(2,1)} %param.9) | copy-start | bytes 393220
  53.7 62.7 %dynamic-slice-start = ((f32[16384]{0:T(1024)}, s32[]{:T(128)}), f32[2048]{0:T(1024)S(1)}, s32[]{:S(2)}) async-start(f32[16384]{0:T(1024)} %param.10, s32[]{:T(128)} %select_n.18), calls=%async_computation.4 | async-start | bytes 16896 | tf_op jit(solution)/shard_map/dynamic_slice | solution.py:35
  102.0 23.8 %copy-start.3 = (f32[4096]{0:T(1024)S(1)}, f32[4096]{0:T(1024)}, u32[]{:S(2)}) copy-start(f32[4096]{0:T(1024)} %param.12) | copy-start | bytes 49156
  118.1 7.8 %all-to-all-start = ((bf16[32,4,512]{2,0,1:T(8,128)(2,1)}), bf16[32,4,512]{2,0,1:T(8,128)(2,1)S(1)}, u32[]{:S(2)}, u32[]{:S(2)}) async-start(bf16[32,4,512]{2,0,1:T(8,128)(2,1)} %bitcast.10), calls=%async_computation.1 | async-start | bytes 262144 | tf_op jit(solution)/shard_map/all_to_all | solution.py:39
  125.9 3.8 %copy-start = (bf16[4096,512]{1,0:T(8,128)(2,1)S(1)}, bf16[4096,512]{1,0:T(8,128)(2,1)}, u32[]{:S(2)}) copy-start(bf16[4096,512]{1,0:T(8,128)(2,1)} %param.13) | copy-start | bytes 12582916
Sparse Core Ops, SparseCore 0:
  37.3 63.4 all-gather.2
Sparse Core Ops, SparseCore 1:
  53.7 34.9 reduce-scatter.1
